TPU v7x, 32 devices: a whole 2x2x4 slice. The times are simulated.
32 devices in a mesh: sample: 4 (over y, x), space: 8 (over z, core).
Axes of the slice: x: 2, y: 2, z: 4, core: 2. Of those that a mesh axis runs over, the one named last changes fastest.
Arguments:
- volume: bfloat16 [4, 16, 16, 4096], P('sample', 'space'), may hold values from -6 to 6
- weight_three: bfloat16 [3, 3, 3, 32, 64], replicated, may hold values from -0.21875 to 0.21875
- bias_three: float32 [64], replicated, may hold values from -3 to 3
- weight_four: bfloat16 [3, 3, 3, 64, 128], replicated, may hold values from -0.15625 to 0.15625
- bias_four: float32 [128], replicated, may hold values from -3 to 3
- cotangent: bfloat16 [4, 16, 4096], P('sample', 'space'), may hold values from -48 to 48
Outputs:
- grad_volume: bfloat16 [4, 16, 16, 4096], P('sample', 'space')
- grad_weight_three: float32 [3, 3, 3, 32, 64], replicated
- grad_bias_three: float32 [64], replicated
- grad_weight_four: float32 [3, 3, 3, 64, 128], replicated
- grad_bias_four: float32 [128], replicated
All inputs are finite; a program needn't handle non-finite values.
Results may differ from a plain program's by a relative error of at most 0.0065.
Values may be sent and summed in bfloat16 or wider, within the bound.
A program may use at most 64 MiB of HBM per device.

v0:
```python
import functools

import jax
import jax.numpy as jnp
from jax import lax
from jax.experimental import pallas as pl
from jax.experimental.pallas import tpu as pltpu
from jax.sharding import PartitionSpec as P

F32 = jnp.float32
BF16 = jnp.bfloat16
MESH = pl.DeviceIdType.MESH
LANES = 128


def slot_of(cell, cells, chans, main, low_side):
    if cell < 0:
        return main + low_side
    if cell == cells:
        return main
    return cell * chans


def place_forward(wide, fwd, low_in):
    cin, cout = wide.shape[1], wide.shape[2]
    fwd[...] = jnp.zeros(fwd.shape, fwd.dtype)
    for tap in range(9):
        for dx in range(3):
            for c in range(LANES // cin):
                row = tap * 2 * LANES + slot_of(c + dx - 1, LANES // cin, cin, LANES, low_in)
                fwd[row : row + cin, c * cout : (c + 1) * cout] = wide[tap * 3 + dx]


def place_back(wide, back, low_out):
    cin, cout = wide.shape[1], wide.shape[2]
    back[...] = jnp.zeros(back.shape, back.dtype)
    for tap in range(9):
        for dx in range(3):
            for c in range(LANES // cin):
                col = tap * (back.shape[1] // 9)
                col += slot_of(c - dx + 1, LANES // cin, cout, 2 * LANES, low_out)
                back[c * cin : (c + 1) * cin, col : col + cout] = wide[(8 - tap) * 3 + dx]


def spread(raw, dst):
    for g in range(dst.shape[1]):
        dst[:, g, :] = raw[:, g * LANES : (g + 1) * LANES].astype(F32)


def neighbours(low, high, groups):
    rows = low.shape[0]
    place = lax.broadcasted_iota(jnp.int32, low.shape, 0) % groups
    right = jnp.where(place == groups - 1, 0.0, pltpu.roll(low, rows - 1, 0))
    left = jnp.where(place == 0, 0.0, pltpu.roll(high, 1, 0))
    return right, left


def widen(plane, first, last):
    h, g, lanes = plane.shape
    flat = plane.astype(F32).reshape(h * g, lanes)
    right, left = neighbours(flat[:, :LANES], flat[:, lanes - LANES :], g)
    if first == LANES:
        side = jnp.concatenate([right, left], axis=1)
    else:
        lane = lax.broadcasted_iota(jnp.int32, right.shape, 1)
        side = jnp.where(lane < first, right, jnp.where(lane >= last, left, 0.0))
    return jnp.concatenate([plane.astype(BF16), side.astype(BF16).reshape(h, g, -1)], axis=2)


def fill(ext, plane, e, first, last):
    height = ext.shape[1] - 2
    edge = jnp.zeros(ext.shape[2:], ext.dtype)
    ext[e, 0] = edge
    ext[e, height + 1] = edge
    ext[e, 1 : height + 1] = widen(plane, first, last)


def window(ext, d, h0, rows, steps=(0, 1, 2)):
    parts = [
        ext[d + dz, pl.ds(h0 + dy, rows)].reshape(-1, ext.shape[3])
        for dz in steps
        for dy in range(3)
    ]
    return jnp.concatenate(parts, axis=1)


def of_steps(steps, unit):
    return pl.ds(steps[0] * 3 * unit, len(steps) * 3 * unit)


def split_steps(d, depth):
    own = [dz for dz in range(3) if 1 <= d + dz <= depth]
    return own, [dz for dz in range(3) if dz not in own]


def nt(a, b):
    return lax.dot_general(a, b, (((1,), (1,)), ((), ())), preferred_element_type=F32)


def slope(v):
    s = jax.nn.sigmoid(v)
    return s * (1.0 + v * (1.0 - s))


def first_own(vol, w, pre, ext):
    depth, height, g, _ = vol.shape
    for d in range(depth):
        fill(ext, vol[d], d + 1, 32, 96)
    step = 8

    @pl.loop(0, height // step)
    def _(block):
        h0 = block * step
        for d in range(depth):
            own, _ = split_steps(d, depth)
            left = window(ext, d, h0, step, own)
            value = jnp.dot(left, w[of_steps(own, ext.shape[3])], preferred_element_type=F32)
            pre[d, pl.ds(h0, step)] = value.reshape(step, g, -1)


def first_kernel(low, high, w, bias, pre, pooled, ext):
    depth, height, g, _ = pre.shape
    fill(ext, low[0], 0, 32, 96)
    fill(ext, high[0], depth + 1, 32, 96)
    step = 8

    @pl.loop(0, height // step)
    def _(block):
        h0 = block * step
        total = 0.0
        for d in range(depth):
            value = pre[d, pl.ds(h0, step)].reshape(step * g, -1) + bias[...]
            _, rest = split_steps(d, depth)
            for dz in rest:
                left = window(ext, d, h0, step, [dz])
                value = value + jnp.dot(
                    left, w[of_steps([dz], ext.shape[3])], preferred_element_type=F32
                )
            pre[d, pl.ds(h0, step)] = value.reshape(step, g, -1)
            total = total + value * jax.nn.sigmoid(value)
        total = jnp.sum(total.reshape(step // 2, 2, g, -1), axis=1).reshape(step // 2 * g, -1)
        a, b = total[:, :LANES], total[:, LANES:]
        lane = lax.broadcasted_iota(jnp.int32, a.shape, 1)
        half = LANES // 2
        mean = jnp.where(lane < half, a + pltpu.roll(a, half, 1), b + pltpu.roll(b, half, 1))
        pooled[pl.ds(block * (step // 2), step // 2)] = (
            (mean * 0.125).astype(BF16).reshape(step // 2, g, LANES)
        )


def second_kernel(pooled, low, high, w, bias, cot, grad, bsum, ext):
    height, g, _ = pooled.shape
    fill(ext, low[...], 0, 64, 64)
    fill(ext, high[...], 2, 64, 64)
    pre = jnp.dot(window(ext, 0, 0, height), w[...], preferred_element_type=F32) + bias[...]
    up = cot[...]
    up = jnp.broadcast_to(up[:, None], (height // 2, 2, g, LANES)).reshape(height * g, LANES)
    up = jnp.concatenate([up, up], axis=1) * 0.125
    value = (up * slope(pre)).astype(BF16)
    grad[...] = value.reshape(grad.shape)
    total = jnp.sum(value.astype(F32), axis=0, keepdims=True)
    bsum[0:1] = total[:, :LANES] + total[:, LANES:]


def tn(a, b):
    return lax.dot_general(a, b, (((0,), (0,)), ((), ())), preferred_element_type=F32)


def keep(buf, piece, rows):
    _, samples, chips, per, _ = buf.shape
    for k in range(rows.shape[0] // 16):
        first = (piece + k) * 16
        chunk, row = first // per, first % per
        core, rest = divmod(chunk, samples * chips)
        buf[core, rest // chips, rest % chips, row : row + 16] = rows[k * 16 : k * 16 + 16]


def kept(buf, piece):
    _, samples, chips, per, _ = buf.shape
    chunk, row = piece * 16 // per, piece * 16 % per
    core, rest = divmod(chunk, samples * chips)
    return buf[core, rest // chips, rest % chips, row : row + 16]


def wgrad_four(ext, grad, buf):
    height = grad.shape[0]
    up = grad[...].reshape(-1, 2 * LANES)
    for tap in range(9):
        part = tn(ext[tap // 3, tap % 3 : tap % 3 + height].reshape(-1, 2 * LANES), up)
        for dx in range(3):
            total = 0.0
            for c in range(2):
                row = slot_of(c + dx - 1, 2, 64, LANES, 64)
                total = total + part[row : row + 64, c * LANES : (c + 1) * LANES]
            keep(buf, (tap * 3 + dx) * 4, total.astype(BF16))


def wgrad_three(ext, grad, buf):
    depth, height = grad.shape[:2]
    for tap in range(9):
        part = 0.0
        for d in range(depth):
            part = part + tn(
                ext[tap // 3 + d, tap % 3 : tap % 3 + height].reshape(-1, 2 * LANES),
                grad[d].reshape(-1, 2 * LANES),
            )
        for dx in range(3):
            even, odd = 0.0, 0.0
            for c in range(4):
                row = slot_of(c + dx - 1, 4, 32, LANES, 96)
                piece = part[row : row + 32, c // 2 * LANES : (c // 2 + 1) * LANES]
                if c % 2:
                    odd = odd + piece
                else:
                    even = even + piece
            total = even + pltpu.roll(odd, 64, 1)
            lane = lax.broadcasted_iota(jnp.int32, (16, LANES), 1)
            packed = jnp.where(lane < 64, total[:16], pltpu.roll(total[16:], 64, 1))
            keep(buf, tap * 3 + dx, packed.astype(BF16))


def third_own(grad, w, part, ext):
    height = grad.shape[0]
    fill(ext, grad[...], 1, LANES, LANES)
    part[...] = nt(window(ext, 0, 0, height, [1]), w[:, of_steps([1], ext.shape[3])])


def third_kernel(low, high, w, part, pre, out, bsum, ext):
    height, g, _ = low.shape
    fill(ext, low[...], 0, LANES, LANES)
    fill(ext, high[...], 2, LANES, LANES)
    back = part[...]
    for dz in (0, 2):
        back = back + nt(window(ext, 0, 0, height, [dz]), w[:, of_steps([dz], ext.shape[3])])
    back = back * 0.125
    turned = pltpu.roll(back, 64, 1)
    lane = lax.broadcasted_iota(jnp.int32, back.shape, 1)
    up = jnp.concatenate(
        [jnp.where(lane < 64, back, turned), jnp.where(lane < 64, turned, back)], axis=1
    ).reshape(height, g, 2 * LANES)
    total = 0.0
    for d in range(pre.shape[0]):
        for h in range(height):
            value = (up[h][None] * slope(pre[d, 2 * h : 2 * h + 2])).astype(BF16)
            out[d, 2 * h : 2 * h + 2] = value
            total = total + jnp.sum(value.astype(F32), axis=0)
    total = jnp.sum(total, axis=0, keepdims=True)
    total = total[:, :LANES] + total[:, LANES:]
    bsum[1:2] = total + pltpu.roll(total, 64, 1)


def fourth_kernel(grad, low, high, w, out, ext):
    depth, height, g, _ = grad.shape
    fill(ext, low[0], 0, 64, 64)
    for d in range(depth):
        fill(ext, grad[d], d + 1, 64, 64)
    fill(ext, high[0], depth + 1, 64, 64)
    step = 8

    @pl.loop(0, height // step)
    def _(block):
        h0 = block * step
        for d in range(depth):
            value = nt(window(ext, d, h0, step), w[...])
            out[d, pl.ds(h0, step)] = value.reshape(step, g, LANES)


class Reduce:
    def __init__(self, net, buf, out, got_a, acc, got_b, mid, got_c):
        self.net = net
        self.buf, self.out = buf, out
        self.got_a, self.acc, self.got_b, self.mid, self.got_c = got_a, acc, got_b, mid, got_c

    def pair(self):
        n = self.net
        self.copies = [n.move(self.buf.at[1 - n.core], self.got_a, n.other)]

    def end(self):
        for copy in self.copies:
            copy.wait()

    def samples(self):
        n = self.net
        self.end()
        self.acc[...] = (self.buf[n.core].astype(F32) + self.got_a[...].astype(F32)).astype(BF16)
        self.copies = [
            n.move(self.acc.at[to[0]], self.got_b.at[j], to) for j, to in enumerate(n.peers)
        ]

    def chips(self):
        n = self.net
        total = self.acc[n.s].astype(F32)
        for j, copy in enumerate(self.copies):
            copy.wait()
            total = total + self.got_b[j].astype(F32)
        self.mid[...] = total.astype(BF16)
        self.copies = [
            n.move(self.mid.at[chip], self.got_c.at[j], to)
            for j, (chip, to) in enumerate(n.line)
        ]

    def back_chips(self):
        n = self.net
        total = self.mid[n.chip].astype(F32)
        for j, copy in enumerate(self.copies):
            copy.wait()
            total = total + self.got_c[j].astype(F32)
        here = self.out.at[n.core, n.s, n.chip]
        here[...] = total.astype(BF16)
        self.copies = [n.move(here, here, to) for _, to in n.line]
        self.wide = [[n.move(here, here, to)] for to in n.peers]

    def back_samples(self):
        n = self.net
        chips = len(n.line) + 1
        for j, copy in enumerate(self.copies):
            copy.wait()
            source = lax.rem(n.chip + chips - 1 - j, chips)
            here = self.out.at[n.core, n.s, source]
            for k, to in enumerate(n.peers):
                self.wide[k].append(n.move(here, here, to))

    def back_pair(self):
        n = self.net
        here = self.out.at[n.core, n.s]
        self.copies = [n.move(here, here, n.other)]
        samples = len(n.peers) + 1
        for k, group in enumerate(self.wide):
            for copy in group:
                copy.wait()
            here = self.out.at[n.core, lax.rem(n.s + samples - 1 - k, samples)]
            self.copies.append(n.move(here, here, n.other))


class Net:
    def __init__(self, samples, space, send, recv):
        self.count = 0
        self.send, self.recv = send, recv
        self.space = space
        self.s = lax.axis_index("sample")
        self.p = lax.axis_index("space")
        self.core = lax.rem(self.p, 2)
        self.chip = lax.div(self.p, 2)
        self.other = (self.s, self.chip * 2 + 1 - self.core)
        self.peers = [(lax.rem(self.s + j, samples), self.p) for j in range(1, samples)]
        self.line = []
        for j in range(1, space // 2):
            to = lax.rem(self.chip + j, space // 2)
            self.line.append((to, (self.s, to * 2 + self.core)))
        self.has_low = self.p > 0
        self.has_high = self.p < space - 1
        self.above = (self.s, lax.rem(self.p + 1, space))
        self.below = (self.s, lax.rem(self.p + space - 1, space))

    def greet(self):
        barrier = pltpu.get_barrier_semaphore()

        def signal(to):
            pl.semaphore_signal(barrier, inc=1, device_id=to, device_id_type=MESH)

        for to in [self.above, self.below, self.other, *self.peers, *[to for _, to in self.line]]:
            signal(to)

    def met(self):
        barrier = pltpu.get_barrier_semaphore()
        pl.semaphore_wait(barrier, 3 + len(self.peers) + len(self.line))

    def make(self, src, dst, to):
        copy = pltpu.make_async_remote_copy(
            src_ref=src,
            dst_ref=dst,
            send_sem=self.send.at[self.count],
            recv_sem=self.recv.at[self.count],
            device_id=to,
            device_id_type=MESH,
        )
        self.count += 1
        return copy

    def move(self, src, dst, to):
        copy = self.make(src, dst, to)
        copy.start()
        return copy

    def halo(self, first, last, low, high):
        up = self.make(last, low, self.above)
        down = self.make(first, high, self.below)

        @pl.when(self.has_high)
        def _():
            up.start()

        @pl.when(self.has_low)
        def _():
            down.start()

        @pl.when(self.p == 0)
        def _():
            low[...] = jnp.zeros(low.shape, low.dtype)

        @pl.when(self.p == self.space - 1)
        def _():
            high[...] = jnp.zeros(high.shape, high.dtype)

        def finish():
            @pl.when(self.has_high)
            def _():
                up.wait_send()
                down.wait_recv()

            @pl.when(self.has_low)
            def _():
                down.wait_send()
                up.wait_recv()

        return finish


def copies_of(samples, space):
    chips = space // 2
    each = 1 + (samples - 1) + 2 * (chips - 1) + chips * (samples - 1) + samples
    return 2 * 4 + 1 + 2 * each + samples + chips


def share(net, rows, gots):
    copy = net.move(rows.at[0], gots[0], net.other)
    yield
    copy.wait()
    rows[1] = rows[0] + gots[0][...]

    def group(src, got, mine, targets):
        copies = [net.move(src, got.at[mine], to) for to in targets]
        got[mine] = src[...]
        return copies

    copies = group(rows.at[1], gots[1], net.s, net.peers)
    yield
    for copy in copies:
        copy.wait()
    rows[2] = jnp.sum(gots[1][...], axis=0)
    copies = group(rows.at[2], gots[2], net.chip, [to for _, to in net.line])
    yield
    for copy in copies:
        copy.wait()
    rows[3] = jnp.sum(gots[2][...], axis=0)
    yield


def mono_kernel(samples, space, *refs):
    vol_hbm, tile_hbm, w3_hbm, w4_hbm, b3_hbm, b4_hbm = refs[:6]
    out, out4, out3, bsum = refs[6:10]
    refs = list(refs[10:])
    w3, w4, fwd3, fwd4, back3, back4 = refs[:6]
    pre, pooled, ext3, grad4, ext4, grad3, wide4, wide3 = refs[6:14]
    halos = refs[14:22]
    other_tile, rows = refs[22:24]
    gots = refs[24:27]
    part4 = refs[27:33]
    part3 = refs[33:39]
    cells, low_cells, high_cells, plane, bias3, bias4 = refs[39:45]
    send, recv, vol, tile, b3, b4, part, here = refs[45:]
    loads = [
        pltpu.make_async_copy(w3_hbm, w3, here.at[0]),
        pltpu.make_async_copy(w4_hbm, w4, here.at[1]),
        pltpu.make_async_copy(vol_hbm, vol, here.at[2]),
        pltpu.make_async_copy(tile_hbm, tile, here.at[3]),
        pltpu.make_async_copy(b3_hbm, b3, here.at[4]),
        pltpu.make_async_copy(b4_hbm, b4, here.at[5]),
    ]
    for load in loads:
        load.start()
    net = Net(samples, space, send, recv)
    net.greet()
    depth = vol.shape[0]
    four = Reduce(net, part4[0], out4, *part4[1:])
    three = Reduce(net, part3[0], out3, *part3[1:])
    loads[0].wait()
    place_forward(w3, fwd3, 96)
    loads[4].wait()
    loads[5].wait()
    for bias, narrow in ((bias3, b3), (bias4, b4)):
        width = narrow.shape[1]
        for c in range(bias.shape[1] // width):
            bias[:, c * width : (c + 1) * width] = narrow[...]
    loads[2].wait()
    loads[3].wait()
    for d in range(depth):
        spread(vol.at[d], cells.at[d])
    net.met()
    done = net.halo(vol.at[0], vol.at[depth - 1], halos[0], halos[1])
    tile_copy = net.move(tile, other_tile, net.other)
    first_own(cells, fwd3, pre, ext3)
    done()
    spread(halos[0], low_cells.at[0])
    spread(halos[1], high_cells.at[0])
    first_kernel(low_cells, high_cells, fwd3, bias3, pre, pooled, ext3)
    done = net.halo(pooled, pooled, halos[2], halos[3])
    fill(ext4, pooled[...], 1, 64, 64)
    loads[1].wait()
    place_forward(w4, fwd4, 64)
    place_back(w4, back4, 128)
    tile_copy.wait()
    odd = net.core == 1
    mine, theirs = tile[...].astype(F32), other_tile[...].astype(F32)
    spread(jnp.where(odd, theirs, mine), plane.at[: tile.shape[0]])
    spread(jnp.where(odd, mine, theirs), plane.at[tile.shape[0] :])
    rows[...] = jnp.zeros(rows.shape, F32)
    four.buf[...] = jnp.zeros(four.buf.shape, BF16)
    three.buf[...] = jnp.zeros(three.buf.shape, BF16)
    done()
    second_kernel(pooled, halos[2], halos[3], fwd4, bias4, plane, grad4, rows.at[0], ext4)
    done = net.halo(grad4, grad4, halos[4], halos[5])
    wgrad_four(ext4, grad4, four.buf)
    four.pair()
    third_own(grad4, back4, part, wide4)
    place_back(w3, back3, 64)
    four.samples()
    done()
    third_kernel(halos[4], halos[5], back4, part, pre, grad3, rows.at[0], wide4)
    done = net.halo(grad3.at[0], grad3.at[depth - 1], halos[6].at[0], halos[7].at[0])
    bias_steps = share(net, rows, gots)
    next(bias_steps)
    wgrad_three(ext3, grad3, three.buf)
    three.pair()
    four.chips()
    next(bias_steps)
    three.samples()
    done()
    fourth_kernel(grad3, halos[6], halos[7], back3, cells, wide3)
    next(bias_steps)
    three.chips()
    four.back_chips()
    for d in range(depth):
        for g in range(cells.shape[2]):
            out[d, :, g * LANES : (g + 1) * LANES] = cells[d, :, g, :].astype(BF16)
    three.back_chips()
    next(bias_steps)
    bsum[...] = rows[3]
    four.back_samples()
    three.back_samples()
    four.back_pair()
    three.back_pair()
    four.end()
    three.end()


def finish_kernel(grad, out4, out3, bsum, volume, wsum3, wsum4, bsum3, bsum4):
    volume[...] = grad[...]
    for t in range(27):
        for k in range(4):
            wsum4[t, k * 16 : k * 16 + 16] = kept(out4, t * 4 + k).astype(F32)
        value = kept(out3, t).astype(F32)
        wsum3[t, :16] = value[:, :64]
        wsum3[t, 16:] = pltpu.roll(value, 64, 1)[:, :64]
    bsum4[...] = bsum[0:1]
    bsum3[...] = bsum[1:2, : bsum3.shape[1]]


def per_of(samples, chips, rows):
    per = 16
    while per * 2 * samples * chips < rows:
        per *= 2
    return per


def parts(samples, chips, rows):
    per = per_of(samples, chips, rows)
    return [
        pltpu.VMEM((2, samples, chips, per, LANES), BF16),
        pltpu.VMEM((samples, chips, per, LANES), BF16),
        pltpu.VMEM((samples, chips, per, LANES), BF16),
        pltpu.VMEM((max(samples - 1, 1), chips, per, LANES), BF16),
        pltpu.VMEM((chips, per, LANES), BF16),
        pltpu.VMEM((max(chips - 1, 1), per, LANES), BF16),
    ]


def local(volume, weight_three, bias_three, weight_four, bias_four, cotangent):
    cin, mid = weight_three.shape[3:]
    cout = weight_four.shape[4]
    depth, height = volume.shape[1:3]
    groups = volume.shape[3] // LANES
    samples, space = lax.axis_size("sample"), lax.axis_size("space")
    tile = cotangent[0]
    w3 = weight_three.reshape(27, cin, mid)
    w4 = weight_four.reshape(27, mid, cout)
    wide = 2 * LANES
    half = height // 2
    shape = jax.ShapeDtypeStruct
    vm = pltpu.VMEM
    copies = copies_of(samples, space)
    vmem = pl.BlockSpec(memory_space=pltpu.VMEM)
    far = pl.BlockSpec(memory_space=pltpu.HBM)
    packed = [
        shape((2, samples, space // 2, per_of(samples, space // 2, n), LANES), BF16)
        for n in (27 * mid, 27 * cin // 2)
    ]
    raw = shape(volume.shape[1:], BF16)
    results = pl.pallas_call(
        functools.partial(mono_kernel, samples, space),
        out_shape=[raw, *packed, shape((8, LANES), F32)],
        in_specs=[far] * 6,
        out_specs=[vmem] * 4,
        scratch_shapes=[
            vm(w3.shape, BF16),
            vm(w4.shape, BF16),
            vm((9 * wide, wide), BF16),
            vm((9 * wide, wide), BF16),
            vm((LANES, 9 * 3 * LANES), BF16),
            vm((LANES, 9 * 4 * LANES), BF16),
            vm((depth, height, groups, wide), F32),
            vm((half, groups, LANES), BF16),
            vm((depth + 2, height + 2, groups, wide), BF16),
            vm((half, groups, wide), BF16),
            vm((3, half + 2, groups, wide), BF16),
            vm((depth, height, groups, wide), BF16),
            vm((3, half + 2, groups, 4 * LANES), BF16),
            vm((depth + 2, height + 2, groups, 3 * LANES), BF16),
            *[vm(volume.shape[2:], BF16)] * 2,
            *[vm((half, groups, LANES), BF16)] * 2,
            *[vm((half, groups, wide), BF16)] * 2,
            *[vm((1, height, groups, wide), BF16)] * 2,
            vm(tile.shape, BF16),
            vm((4, 8, LANES), F32),
            vm((8, LANES), F32),
            vm((samples, 8, LANES), F32),
            vm((space // 2, 8, LANES), F32),
            *parts(samples, space // 2, 27 * mid),
            *parts(samples, space // 2, 27 * cin // 2),
            vm((depth, height, groups, LANES), F32),
            *[vm((1, height, groups, LANES), F32)] * 2,
            vm((2 * tile.shape[0], groups, LANES), F32),
            vm((1, wide), F32),
            vm((1, wide), F32),
            pltpu.SemaphoreType.DMA((copies,)),
            pltpu.SemaphoreType.DMA((copies,)),
            vm(volume.shape[1:], BF16),
            vm(tile.shape, BF16),
            vm((1, mid), F32),
            vm((1, cout), F32),
            vm((half * groups, LANES), F32),
            pltpu.SemaphoreType.DMA((6,)),
        ],
        compiler_params=pltpu.CompilerParams(
            collective_id=0, has_side_effects=True, vmem_limit_bytes=36 * 2**20
        ),
    )(
        *[
            pltpu.with_memory_space_constraint(a, pltpu.HBM)
            for a in (volume[0], tile, w3, w4, bias_three[None], bias_four[None])
        ]
    )
    grad_field, wsum_three, wsum_four, bsum_three, bsum_four = pl.pallas_call(
        finish_kernel,
        out_shape=[
            raw,
            shape((27, cin, mid), F32),
            shape((27, mid, cout), F32),
            shape((1, mid), F32),
            shape((1, cout), F32),
        ],
        in_specs=[vmem] * 4,
        out_specs=[vmem] * 5,
        compiler_params=pltpu.CompilerParams(vmem_limit_bytes=16 * 2**20),
    )(*results)
    return (
        grad_field.reshape(volume.shape),
        wsum_three.reshape(weight_three.shape),
        bsum_three[0],
        wsum_four.reshape(weight_four.shape),
        bsum_four[0],
    )


def solution(mesh):
    placed = (P("sample", "space", None, None), P(), P(), P(), P(), P("sample", "space", None))
    return jax.shard_map(
        local,
        mesh=mesh,
        in_specs=placed,
        out_specs=(P("sample", "space", None, None), P(), P(), P(), P()),
        check_vma=False,
    )
```

profile of v0, /device:TPU:0, one launch (start us, length us, event | category | flops | bytes accessed | tf_op | source)
XLA Modules:
  0.0 42.1 jit_solution(9174518742113334165)
XLA Ops:
  0.6 40.2 %shard_map.101 = (bf16[2,16,4096]{2,1,0:T(8,128)(2,1)S(1)}, bf16[2,4,4,64,128]{4,3,2,1,0:T(8,128)(2,1)S(1)}, bf16[2,4,4,16,128]{4,3,2,1,0:T(8,128)(2,1)S(1)}, f32[8,128]{1,0:T(8,128)S(1)}) custom-call(bf16[2,16,4096]{2,1,0:T(8,128)(2,1)} %bitcast.12, bf16[2,4096]{1,0:T(2,128)(2,1)} %bitcast.14, bf16[27,32,64]{2,1,0:T(8,128)(2,1)} %bitcast.13, ...), custom_call_target="tpu_custom_call" | custom-call | tf_op jit(solution)/shard_map/pallas_call | solution.py:599
  40.9 1.2 %shard_map.102 = (bf16[2,16,4096]{2,1,0:T(8,128)(2,1)}, f32[27,32,64]{2,1,0:T(8,128)}, f32[27,64,128]{2,1,0:T(8,128)}, f32[1,64]{1,0:T(1,128)}, f32[1,128]{1,0:T(1,128)}) custom-call(bf16[2,16,4096]{2,1,0:T(8,128)(2,1)S(1)} %get-tuple-element.14.grad, bf16[2,4,4,64,128]{4,3,2,1,0:T(8,128)(2,1)S(1)} %get-tuple-element.15.out4, ...), custom_call_target="tpu_custom_call" | custom-call | tf_op jit(solution)/shard_map/pallas_call | solution.py:653
where the time goes:
time: 42.2 us; the launch traced here: 42.1 us
  Pallas kernels  41.4 us (98%)
  between operations  0.64 us (2%)
    pallas_call x1, Pallas kernels, local(): pl.pallas_call(functools.partial(mono_kernel, samples, space), out_shape=...  40.2 us
    pallas_call x1, Pallas kernels, local(): pl.pallas_call(finish_kernel, out_shape=[raw, shape((27, cin, mid), F32),...  1.19 us

commit v1 on v0

--- a/solution.py
+++ b/solution.py
@@ -249,20 +249,21 @@
     bsum[1:2] = total + pltpu.roll(total, 64, 1)
 
 
-def fourth_kernel(grad, low, high, w, out, ext):
-    depth, height, g, _ = grad.shape
+def fourth_fill(grad, low, high, ext):
+    depth = grad.shape[0]
     fill(ext, low[0], 0, 64, 64)
     for d in range(depth):
         fill(ext, grad[d], d + 1, 64, 64)
     fill(ext, high[0], depth + 1, 64, 64)
-    step = 8
-
-    @pl.loop(0, height // step)
-    def _(block):
-        h0 = block * step
-        for d in range(depth):
-            value = nt(window(ext, d, h0, step), w[...])
-            out[d, pl.ds(h0, step)] = value.reshape(step, g, LANES)
+
+
+def fourth_part(w, out, ext, block):
+    depth, height, g, _ = out.shape
+    step = height // 2
+    h0 = block * step
+    for d in range(depth):
+        value = nt(window(ext, d, h0, step), w[...])
+        out[d, pl.ds(h0, step)] = value.reshape(step, g, LANES)
 
 
 class Reduce:
@@ -330,6 +331,41 @@
                 copy.wait()
             here = self.out.at[n.core, lax.rem(n.s + samples - 1 - k, samples)]
             self.copies.append(n.move(here, here, n.other))
+
+
+class Gather:
+    def __init__(self, net, buf, out, got_a, field):
+        self.net = net
+        self.buf, self.out, self.got_a, self.field = buf, out, got_a, field
+
+    def scatter(self):
+        n = self.net
+        self.copies = [
+            n.move(self.buf.at[core, s], self.got_a.at[j], to)
+            for j, (core, s, to) in enumerate(n.plane)
+        ]
+
+    def along(self):
+        n = self.net
+        total = self.buf[n.core, n.s].astype(F32)
+        for j, copy in enumerate(self.copies):
+            copy.wait()
+            total = total + self.got_a[j].astype(F32)
+        here = self.field.at[n.chip]
+        here[...] = total.astype(BF16)
+        self.copies = [n.move(here, here, to) for _, to in n.line]
+
+    def back(self):
+        n = self.net
+        for copy in self.copies:
+            copy.wait()
+        here = self.out.at[n.core, n.s]
+        here[...] = jnp.sum(self.field[...].astype(F32), axis=0).astype(BF16)
+        self.copies = [n.move(here, here, to) for _, _, to in n.plane]
+
+    def end(self):
+        for copy in self.copies:
+            copy.wait()
 
 
 class Net:
@@ -343,6 +379,12 @@
         self.chip = lax.div(self.p, 2)
         self.other = (self.s, self.chip * 2 + 1 - self.core)
         self.peers = [(lax.rem(self.s + j, samples), self.p) for j in range(1, samples)]
+        self.plane = []
+        for j in range(samples - 1, -1, -1):
+            for k in (1, 0):
+                if j or k:
+                    s, core = lax.rem(self.s + j, samples), lax.rem(self.core + k, 2)
+                    self.plane.append((core, s, (s, self.chip * 2 + core)))
         self.line = []
         for j in range(1, space // 2):
             to = lax.rem(self.chip + j, space // 2)
@@ -358,12 +400,16 @@
         def signal(to):
             pl.semaphore_signal(barrier, inc=1, device_id=to, device_id_type=MESH)
 
-        for to in [self.above, self.below, self.other, *self.peers, *[to for _, to in self.line]]:
+        for to in [self.above, self.below]:
+            signal(to)
+        for _, _, to in self.plane:
+            signal(to)
+        for _, to in self.line:
             signal(to)
 
     def met(self):
         barrier = pltpu.get_barrier_semaphore()
-        pl.semaphore_wait(barrier, 3 + len(self.peers) + len(self.line))
+        pl.semaphore_wait(barrier, 2 + len(self.plane) + len(self.line))
 
     def make(self, src, dst, to):
         copy = pltpu.make_async_remote_copy(
@@ -418,31 +464,29 @@
 
 def copies_of(samples, space):
     chips = space // 2
-    each = 1 + (samples - 1) + 2 * (chips - 1) + chips * (samples - 1) + samples
-    return 2 * 4 + 1 + 2 * each + samples + chips
+    four = 1 + (samples - 1) + 2 * (chips - 1) + chips * (samples - 1) + samples
+    flat, line = 2 * samples - 1, chips - 1
+    return 2 * 4 + 1 + four + 2 * flat + line + flat + line
 
 
 def share(net, rows, gots):
-    copy = net.move(rows.at[0], gots[0], net.other)
-    yield
-    copy.wait()
-    rows[1] = rows[0] + gots[0][...]
-
     def group(src, got, mine, targets):
         copies = [net.move(src, got.at[mine], to) for to in targets]
         got[mine] = src[...]
         return copies
 
-    copies = group(rows.at[1], gots[1], net.s, net.peers)
+    samples = gots[0].shape[0] // 2
+    mine = net.core * samples + net.s
+    copies = group(rows.at[0], gots[0], mine, [to for _, _, to in net.plane])
+    yield
+    for copy in copies:
+        copy.wait()
+    rows[1] = jnp.sum(gots[0][...], axis=0)
+    copies = group(rows.at[1], gots[1], net.chip, [to for _, to in net.line])
     yield
     for copy in copies:
         copy.wait()
     rows[2] = jnp.sum(gots[1][...], axis=0)
-    copies = group(rows.at[2], gots[2], net.chip, [to for _, to in net.line])
-    yield
-    for copy in copies:
-        copy.wait()
-    rows[3] = jnp.sum(gots[2][...], axis=0)
     yield
 
 
@@ -454,18 +498,18 @@
     pre, pooled, ext3, grad4, ext4, grad3, wide4, wide3 = refs[6:14]
     halos = refs[14:22]
     other_tile, rows = refs[22:24]
-    gots = refs[24:27]
-    part4 = refs[27:33]
-    part3 = refs[33:39]
-    cells, low_cells, high_cells, plane, bias3, bias4 = refs[39:45]
-    send, recv, vol, tile, b3, b4, part, here = refs[45:]
+    gots = refs[24:26]
+    part4 = refs[26:32]
+    part3 = refs[32:35]
+    cells, low_cells, high_cells, plane, bias3, bias4 = refs[35:41]
+    send, recv, vol, tile, b3, b4, part, here = refs[41:]
     loads = [
         pltpu.make_async_copy(w3_hbm, w3, here.at[0]),
-        pltpu.make_async_copy(w4_hbm, w4, here.at[1]),
         pltpu.make_async_copy(vol_hbm, vol, here.at[2]),
-        pltpu.make_async_copy(tile_hbm, tile, here.at[3]),
         pltpu.make_async_copy(b3_hbm, b3, here.at[4]),
         pltpu.make_async_copy(b4_hbm, b4, here.at[5]),
+        pltpu.make_async_copy(w4_hbm, w4, here.at[1]),
+        pltpu.make_async_copy(tile_hbm, tile, here.at[3]),
     ]
     for load in loads:
         load.start()
@@ -473,22 +517,21 @@
     net.greet()
     depth = vol.shape[0]
     four = Reduce(net, part4[0], out4, *part4[1:])
-    three = Reduce(net, part3[0], out3, *part3[1:])
+    three = Gather(net, part3[0], out3, *part3[1:])
+    net.met()
+    done = net.halo(vol_hbm.at[0], vol_hbm.at[depth - 1], halos[0], halos[1])
+    tile_copy = net.move(tile_hbm, other_tile, net.other)
     loads[0].wait()
     place_forward(w3, fwd3, 96)
-    loads[4].wait()
-    loads[5].wait()
+    loads[2].wait()
+    loads[3].wait()
     for bias, narrow in ((bias3, b3), (bias4, b4)):
         width = narrow.shape[1]
         for c in range(bias.shape[1] // width):
             bias[:, c * width : (c + 1) * width] = narrow[...]
-    loads[2].wait()
-    loads[3].wait()
+    loads[1].wait()
     for d in range(depth):
         spread(vol.at[d], cells.at[d])
-    net.met()
-    done = net.halo(vol.at[0], vol.at[depth - 1], halos[0], halos[1])
-    tile_copy = net.move(tile, other_tile, net.other)
     first_own(cells, fwd3, pre, ext3)
     done()
     spread(halos[0], low_cells.at[0])
@@ -496,9 +539,11 @@
     first_kernel(low_cells, high_cells, fwd3, bias3, pre, pooled, ext3)
     done = net.halo(pooled, pooled, halos[2], halos[3])
     fill(ext4, pooled[...], 1, 64, 64)
-    loads[1].wait()
+    loads[4].wait()
     place_forward(w4, fwd4, 64)
     place_back(w4, back4, 128)
+    place_back(w3, back3, 64)
+    loads[5].wait()
     tile_copy.wait()
     odd = net.core == 1
     mine, theirs = tile[...].astype(F32), other_tile[...].astype(F32)
@@ -513,7 +558,6 @@
     wgrad_four(ext4, grad4, four.buf)
     four.pair()
     third_own(grad4, back4, part, wide4)
-    place_back(w3, back3, 64)
     four.samples()
     done()
     third_kernel(halos[4], halos[5], back4, part, pre, grad3, rows.at[0], wide4)
@@ -521,25 +565,23 @@
     bias_steps = share(net, rows, gots)
     next(bias_steps)
     wgrad_three(ext3, grad3, three.buf)
-    three.pair()
+    three.scatter()
     four.chips()
     next(bias_steps)
-    three.samples()
     done()
-    fourth_kernel(grad3, halos[6], halos[7], back3, cells, wide3)
+    fourth_fill(grad3, halos[6], halos[7], wide3)
+    fourth_part(back3, cells, wide3, 0)
+    three.along()
+    four.back_chips()
     next(bias_steps)
-    three.chips()
-    four.back_chips()
+    fourth_part(back3, cells, wide3, 1)
     for d in range(depth):
         for g in range(cells.shape[2]):
             out[d, :, g * LANES : (g + 1) * LANES] = cells[d, :, g, :].astype(BF16)
-    three.back_chips()
-    next(bias_steps)
-    bsum[...] = rows[3]
+    bsum[...] = rows[2]
     four.back_samples()
-    three.back_samples()
+    three.back()
     four.back_pair()
-    three.back_pair()
     four.end()
     three.end()
 
@@ -572,6 +614,15 @@
         pltpu.VMEM((max(samples - 1, 1), chips, per, LANES), BF16),
         pltpu.VMEM((chips, per, LANES), BF16),
         pltpu.VMEM((max(chips - 1, 1), per, LANES), BF16),
+    ]
+
+
+def pieces(samples, chips, rows):
+    per = per_of(samples, 1, rows)
+    return [
+        pltpu.VMEM((2, samples, 1, per, LANES), BF16),
+        pltpu.VMEM((2 * samples - 1, 1, per, LANES), BF16),
+        pltpu.VMEM((chips, 1, per, LANES), BF16),
     ]
 
 
@@ -592,8 +643,8 @@
     vmem = pl.BlockSpec(memory_space=pltpu.VMEM)
     far = pl.BlockSpec(memory_space=pltpu.HBM)
     packed = [
-        shape((2, samples, space // 2, per_of(samples, space // 2, n), LANES), BF16)
-        for n in (27 * mid, 27 * cin // 2)
+        shape((2, samples, chips, per_of(samples, chips, n), LANES), BF16)
+        for chips, n in ((space // 2, 27 * mid), (1, 27 * cin // 2))
     ]
     raw = shape(volume.shape[1:], BF16)
     results = pl.pallas_call(
@@ -621,12 +672,11 @@
             *[vm((half, groups, wide), BF16)] * 2,
             *[vm((1, height, groups, wide), BF16)] * 2,
             vm(tile.shape, BF16),
-            vm((4, 8, LANES), F32),
-            vm((8, LANES), F32),
-            vm((samples, 8, LANES), F32),
+            vm((3, 8, LANES), F32),
+            vm((2 * samples, 8, LANES), F32),
             vm((space // 2, 8, LANES), F32),
             *parts(samples, space // 2, 27 * mid),
-            *parts(samples, space // 2, 27 * cin // 2),
+            *pieces(samples, space // 2, 27 * cin // 2),
             vm((depth, height, groups, LANES), F32),
             *[vm((1, height, groups, LANES), F32)] * 2,
             vm((2 * tile.shape[0], groups, LANES), F32),

time: 42.2 us -> 39 us (0.924)
  Pallas kernels: 41.4 us -> 38.2 us
    pallas_call x1, Pallas kernels: 40.2 us -> 37 us  [local(): pl.pallas_call(functools.partial(mono_kernel, samples, space), out_shape=...]
where the time goes in v1:
time: 39 us; the launch traced here: 38.8 us
  Pallas kernels  38.2 us (98%)
  between operations  0.64 us (2%)
    pallas_call x1, Pallas kernels, local(): pl.pallas_call(functools.partial(mono_kernel, samples, space), out_shape=...  37 us
    pallas_call x1, Pallas kernels, local(): pl.pallas_call(finish_kernel, out_shape=[raw, shape((27, cin, mid), F32),...  1.19 us

profile of v1, /device:TPU:0, one launch (start us, length us, event | category | flops | bytes accessed | tf_op | source)
XLA Modules:
  0.0 38.8 jit_solution(17075086823568630644)
XLA Ops:
  0.6 37.0 %shard_map.101 = (bf16[2,16,4096]{2,1,0:T(8,128)(2,1)S(1)}, bf16[2,4,4,64,128]{4,3,2,1,0:T(8,128)(2,1)S(1)}, bf16[2,4,1,64,128]{4,3,2,1,0:T(8,128)(2,1)S(1)}, f32[8,128]{1,0:T(8,128)S(1)}) custom-call(bf16[2,16,4096]{2,1,0:T(8,128)(2,1)} %bitcast.12, bf16[2,4096]{1,0:T(2,128)(2,1)} %bitcast.14, bf16[27,32,64]{2,1,0:T(8,128)(2,1)} %bitcast.13, ...), custom_call_target="tpu_custom_call" | custom-call | tf_op jit(solution)/shard_map/pallas_call | solution.py:650
  37.6 1.2 %shard_map.102 = (bf16[2,16,4096]{2,1,0:T(8,128)(2,1)}, f32[27,32,64]{2,1,0:T(8,128)}, f32[27,64,128]{2,1,0:T(8,128)}, f32[1,64]{1,0:T(1,128)}, f32[1,128]{1,0:T(1,128)}) custom-call(bf16[2,16,4096]{2,1,0:T(8,128)(2,1)S(1)} %get-tuple-element.14.grad, bf16[2,4,4,64,128]{4,3,2,1,0:T(8,128)(2,1)S(1)} %get-tuple-element.15.out4, ...), custom_call_target="tpu_custom_call" | custom-call | tf_op jit(solution)/shard_map/pallas_call | solution.py:703

commit v2 on v1

--- a/solution.py
+++ b/solution.py
@@ -11,6 +11,7 @@
 BF16 = jnp.bfloat16
 MESH = pl.DeviceIdType.MESH
 LANES = 128
+HALVES = (range(0, 5), range(5, 9))
 
 
 def slot_of(cell, cells, chans, main, low_side):
@@ -148,11 +149,28 @@
         )
 
 
-def second_kernel(pooled, low, high, w, bias, cot, grad, bsum, ext):
-    height, g, _ = pooled.shape
+def slopes(pre):
+    @pl.loop(0, pre.shape[1] // 2)
+    def _(block):
+        for d in range(pre.shape[0]):
+            here = pl.ds(block * 2, 2)
+            pre[d, here] = slope(pre[d, here])
+
+
+def second_own(w, bias, part, ext):
+    height = ext.shape[1] - 2
+    own = w[of_steps([1], ext.shape[3])]
+    part[...] = jnp.dot(window(ext, 0, 0, height, [1]), own, preferred_element_type=F32) + bias[...]
+
+
+def second_kernel(low, high, w, part, cot, grad, bsum, ext):
+    height, g, _ = low.shape
     fill(ext, low[...], 0, 64, 64)
     fill(ext, high[...], 2, 64, 64)
-    pre = jnp.dot(window(ext, 0, 0, height), w[...], preferred_element_type=F32) + bias[...]
+    pre = part[...]
+    for dz in (0, 2):
+        rest = w[of_steps([dz], ext.shape[3])]
+        pre = pre + jnp.dot(window(ext, 0, 0, height, [dz]), rest, preferred_element_type=F32)
     up = cot[...]
     up = jnp.broadcast_to(up[:, None], (height // 2, 2, g, LANES)).reshape(height * g, LANES)
     up = jnp.concatenate([up, up], axis=1) * 0.125
@@ -182,22 +200,22 @@
     return buf[core, rest // chips, rest % chips, row : row + 16]
 
 
-def wgrad_four(ext, grad, buf):
+def wgrad_four(ext, grad, buf, taps):
     height = grad.shape[0]
     up = grad[...].reshape(-1, 2 * LANES)
-    for tap in range(9):
+    for place, tap in enumerate(taps):
         part = tn(ext[tap // 3, tap % 3 : tap % 3 + height].reshape(-1, 2 * LANES), up)
         for dx in range(3):
             total = 0.0
             for c in range(2):
                 row = slot_of(c + dx - 1, 2, 64, LANES, 64)
                 total = total + part[row : row + 64, c * LANES : (c + 1) * LANES]
-            keep(buf, (tap * 3 + dx) * 4, total.astype(BF16))
-
-
-def wgrad_three(ext, grad, buf):
+            keep(buf, (place * 3 + dx) * 4, total.astype(BF16))
+
+
+def wgrad_three(ext, grad, buf, taps):
     depth, height = grad.shape[:2]
-    for tap in range(9):
+    for tap in taps:
         part = 0.0
         for d in range(depth):
             part = part + tn(
@@ -241,7 +259,7 @@
     total = 0.0
     for d in range(pre.shape[0]):
         for h in range(height):
-            value = (up[h][None] * slope(pre[d, 2 * h : 2 * h + 2])).astype(BF16)
+            value = (up[h][None] * pre[d, 2 * h : 2 * h + 2]).astype(BF16)
             out[d, 2 * h : 2 * h + 2] = value
             total = total + jnp.sum(value.astype(F32), axis=0)
     total = jnp.sum(total, axis=0, keepdims=True)
@@ -464,7 +482,7 @@
 
 def copies_of(samples, space):
     chips = space // 2
-    four = 1 + (samples - 1) + 2 * (chips - 1) + chips * (samples - 1) + samples
+    four = 2 * (1 + (samples - 1) + 2 * (chips - 1) + chips * (samples - 1) + samples)
     flat, line = 2 * samples - 1, chips - 1
     return 2 * 4 + 1 + four + 2 * flat + line + flat + line
 
@@ -492,17 +510,17 @@
 
 def mono_kernel(samples, space, *refs):
     vol_hbm, tile_hbm, w3_hbm, w4_hbm, b3_hbm, b4_hbm = refs[:6]
-    out, out4, out3, bsum = refs[6:10]
-    refs = list(refs[10:])
+    out, *outs4, out3, bsum = refs[6:11]
+    refs = list(refs[11:])
     w3, w4, fwd3, fwd4, back3, back4 = refs[:6]
     pre, pooled, ext3, grad4, ext4, grad3, wide4, wide3 = refs[6:14]
     halos = refs[14:22]
     other_tile, rows = refs[22:24]
     gots = refs[24:26]
-    part4 = refs[26:32]
-    part3 = refs[32:35]
-    cells, low_cells, high_cells, plane, bias3, bias4 = refs[35:41]
-    send, recv, vol, tile, b3, b4, part, here = refs[41:]
+    parts4 = refs[26:32], refs[32:38]
+    part3 = refs[38:41]
+    cells, low_cells, high_cells, plane, bias3, bias4 = refs[41:47]
+    send, recv, vol, tile, b3, b4, part, part_fwd, here = refs[47:]
     loads = [
         pltpu.make_async_copy(w3_hbm, w3, here.at[0]),
         pltpu.make_async_copy(vol_hbm, vol, here.at[2]),
@@ -516,7 +534,7 @@
     net = Net(samples, space, send, recv)
     net.greet()
     depth = vol.shape[0]
-    four = Reduce(net, part4[0], out4, *part4[1:])
+    fours = [Reduce(net, p[0], o, *p[1:]) for p, o in zip(parts4, outs4)]
     three = Gather(net, part3[0], out3, *part3[1:])
     net.met()
     done = net.halo(vol_hbm.at[0], vol_hbm.at[depth - 1], halos[0], halos[1])
@@ -541,8 +559,8 @@
     fill(ext4, pooled[...], 1, 64, 64)
     loads[4].wait()
     place_forward(w4, fwd4, 64)
+    second_own(fwd4, bias4, part_fwd, ext4)
     place_back(w4, back4, 128)
-    place_back(w3, back3, 64)
     loads[5].wait()
     tile_copy.wait()
     odd = net.core == 1
@@ -550,47 +568,61 @@
     spread(jnp.where(odd, theirs, mine), plane.at[: tile.shape[0]])
     spread(jnp.where(odd, mine, theirs), plane.at[tile.shape[0] :])
     rows[...] = jnp.zeros(rows.shape, F32)
-    four.buf[...] = jnp.zeros(four.buf.shape, BF16)
-    three.buf[...] = jnp.zeros(three.buf.shape, BF16)
+    for each in (*fours, three):
+        each.buf[...] = jnp.zeros(each.buf.shape, BF16)
+    slopes(pre)
     done()
-    second_kernel(pooled, halos[2], halos[3], fwd4, bias4, plane, grad4, rows.at[0], ext4)
+    second_kernel(halos[2], halos[3], fwd4, part_fwd, plane, grad4, rows.at[0], ext4)
     done = net.halo(grad4, grad4, halos[4], halos[5])
-    wgrad_four(ext4, grad4, four.buf)
-    four.pair()
+    for four, taps in zip(fours, HALVES):
+        wgrad_four(ext4, grad4, four.buf, taps)
+        four.pair()
     third_own(grad4, back4, part, wide4)
-    four.samples()
+    fours[0].samples()
+    place_back(w3, back3, 64)
+    fours[1].samples()
     done()
     third_kernel(halos[4], halos[5], back4, part, pre, grad3, rows.at[0], wide4)
     done = net.halo(grad3.at[0], grad3.at[depth - 1], halos[6].at[0], halos[7].at[0])
     bias_steps = share(net, rows, gots)
     next(bias_steps)
-    wgrad_three(ext3, grad3, three.buf)
+    wgrad_three(ext3, grad3, three.buf, range(0, 3))
+    fours[0].chips()
+    wgrad_three(ext3, grad3, three.buf, range(3, 6))
+    fours[1].chips()
+    wgrad_three(ext3, grad3, three.buf, range(6, 9))
     three.scatter()
-    four.chips()
+    done()
+    fours[0].back_chips()
+    fourth_fill(grad3, halos[6], halos[7], wide3)
+    fours[1].back_chips()
     next(bias_steps)
-    done()
-    fourth_fill(grad3, halos[6], halos[7], wide3)
     fourth_part(back3, cells, wide3, 0)
     three.along()
-    four.back_chips()
     next(bias_steps)
     fourth_part(back3, cells, wide3, 1)
     for d in range(depth):
         for g in range(cells.shape[2]):
             out[d, :, g * LANES : (g + 1) * LANES] = cells[d, :, g, :].astype(BF16)
     bsum[...] = rows[2]
-    four.back_samples()
+    for four in fours:
+        four.back_samples()
     three.back()
-    four.back_pair()
-    four.end()
-    three.end()
-
-
-def finish_kernel(grad, out4, out3, bsum, volume, wsum3, wsum4, bsum3, bsum4):
+    for four in fours:
+        four.back_pair()
+    for each in (*fours, three):
+        each.end()
+
+
+def finish_kernel(grad, out4a, out4b, out3, bsum, volume, wsum3, wsum4, bsum3, bsum4):
     volume[...] = grad[...]
+    for out4, taps in zip((out4a, out4b), HALVES):
+        for place, tap in enumerate(taps):
+            for dx in range(3):
+                for k in range(4):
+                    rows = kept(out4, (place * 3 + dx) * 4 + k)
+                    wsum4[tap * 3 + dx, k * 16 : k * 16 + 16] = rows.astype(F32)
     for t in range(27):
-        for k in range(4):
-            wsum4[t, k * 16 : k * 16 + 16] = kept(out4, t * 4 + k).astype(F32)
         value = kept(out3, t).astype(F32)
         wsum3[t, :16] = value[:, :64]
         wsum3[t, 16:] = pltpu.roll(value, 64, 1)[:, :64]
@@ -642,16 +674,17 @@
     copies = copies_of(samples, space)
     vmem = pl.BlockSpec(memory_space=pltpu.VMEM)
     far = pl.BlockSpec(memory_space=pltpu.HBM)
+    counts = [3 * len(taps) * mid for taps in HALVES]
     packed = [
         shape((2, samples, chips, per_of(samples, chips, n), LANES), BF16)
-        for chips, n in ((space // 2, 27 * mid), (1, 27 * cin // 2))
+        for chips, n in (*[(space // 2, n) for n in counts], (1, 27 * cin // 2))
     ]
     raw = shape(volume.shape[1:], BF16)
     results = pl.pallas_call(
         functools.partial(mono_kernel, samples, space),
         out_shape=[raw, *packed, shape((8, LANES), F32)],
         in_specs=[far] * 6,
-        out_specs=[vmem] * 4,
+        out_specs=[vmem] * 5,
         scratch_shapes=[
             vm(w3.shape, BF16),
             vm(w4.shape, BF16),
@@ -675,7 +708,8 @@
             vm((3, 8, LANES), F32),
             vm((2 * samples, 8, LANES), F32),
             vm((space // 2, 8, LANES), F32),
-            *parts(samples, space // 2, 27 * mid),
+            *parts(samples, space // 2, counts[0]),
+            *parts(samples, space // 2, counts[1]),
             *pieces(samples, space // 2, 27 * cin // 2),
             vm((depth, height, groups, LANES), F32),
             *[vm((1, height, groups, LANES), F32)] * 2,
@@ -689,6 +723,7 @@
             vm((1, mid), F32),
             vm((1, cout), F32),
             vm((half * groups, LANES), F32),
+            vm((half * groups, wide), F32),
             pltpu.SemaphoreType.DMA((6,)),
         ],
         compiler_params=pltpu.CompilerParams(
@@ -709,7 +744,7 @@
             shape((1, mid), F32),
             shape((1, cout), F32),
         ],
-        in_specs=[vmem] * 4,
+        in_specs=[vmem] * 5,
         out_specs=[vmem] * 5,
         compiler_params=pltpu.CompilerParams(vmem_limit_bytes=16 * 2**20),
     )(*results)

time: 39 us -> 40.7 us (1.044)
  Pallas kernels: 38.2 us -> 39.9 us
    pallas_call x1, Pallas kernels: 37 us -> 38.8 us  [local(): pl.pallas_call(functools.partial(mono_kernel, samples, space), out_shape=...]
where the time goes in v2:
time: 40.7 us; the launch traced here: 40.6 us
  Pallas kernels  39.9 us (98%)
  between operations  0.64 us (2%)
    pallas_call x1, Pallas kernels, local(): pl.pallas_call(functools.partial(mono_kernel, samples, space), out_shape=...  38.8 us
    pallas_call x1, Pallas kernels, local(): pl.pallas_call(finish_kernel, out_shape=[raw, shape((27, cin, mid), F32),...  1.19 us

profile of v2, /device:TPU:0, one launch (start us, length us, event | category | flops | bytes accessed | tf_op | source)
XLA Modules:
  0.0 40.6 jit_solution(18426595578275248665)
XLA Ops:
  0.6 38.8 %shard_map.101 = (bf16[2,16,4096]{2,1,0:T(8,128)(2,1)S(1)}, bf16[2,4,4,32,128]{4,3,2,1,0:T(8,128)(2,1)S(1)}, bf16[2,4,4,32,128]{4,3,2,1,0:T(8,128)(2,1)S(1)}, bf...) custom-call(bf16[2,16,4096]{2,1,0:T(8,128)(2,1)} %bitcast.12, bf16[2,4096]{1,0:T(2,128)(2,1)} %bitcast.14, ...), custom_call_target="tpu_custom_call" | custom-call | tf_op jit(solution)/shard_map/pallas_call | solution.py:683
  39.4 1.2 %shard_map.102 = (bf16[2,16,4096]{2,1,0:T(8,128)(2,1)}, f32[27,32,64]{2,1,0:T(8,128)}, f32[27,64,128]{2,1,0:T(8,128)}, f32[1,64]{1,0:T(1,128)}, f32[1,128]{1,0:T(1,128)}) custom-call(bf16[2,16,4096]{2,1,0:T(8,128)(2,1)S(1)} %get-tuple-element.15.grad, bf16[2,4,4,32,128]{4,3,2,1,0:T(8,128)(2,1)S(1)} %get-tuple-element.16.out4a, ...), custom_call_target="tpu_custom_call" | custom-call | tf_op jit(solution)/shard_map/pallas_call | solution.py:738

commit v3 on v2

--- a/solution.py
+++ b/solution.py
@@ -237,19 +237,21 @@
             keep(buf, tap * 3 + dx, packed.astype(BF16))
 
 
-def third_own(grad, w, part, ext):
-    height = grad.shape[0]
-    fill(ext, grad[...], 1, LANES, LANES)
-    part[...] = nt(window(ext, 0, 0, height, [1]), w[:, of_steps([1], ext.shape[3])])
-
-
-def third_kernel(low, high, w, part, pre, out, bsum, ext):
+def third_near(grad, w, first, last, ext):
+    fill(ext, grad[...], 0, LANES, LANES)
+    for dz, side in ((2, first), (0, last)):
+        side[...] = third_step(w, dz, ext).astype(BF16).reshape(side.shape)
+
+
+def third_step(w, dz, ext):
+    return nt(window(ext, -dz, 0, ext.shape[1] - 2, [dz]), w[:, of_steps([dz], ext.shape[3])])
+
+
+def third_kernel(low, high, part, pre, out, bsum):
     height, g, _ = low.shape
-    fill(ext, low[...], 0, LANES, LANES)
-    fill(ext, high[...], 2, LANES, LANES)
     back = part[...]
-    for dz in (0, 2):
-        back = back + nt(window(ext, 0, 0, height, [dz]), w[:, of_steps([dz], ext.shape[3])])
+    for side in (low, high):
+        back = back + side[...].astype(F32).reshape(back.shape)
     back = back * 0.125
     turned = pltpu.roll(back, 64, 1)
     lane = lax.broadcasted_iota(jnp.int32, back.shape, 1)
@@ -267,12 +269,19 @@
     bsum[1:2] = total + pltpu.roll(total, 64, 1)
 
 
-def fourth_fill(grad, low, high, ext):
-    depth = grad.shape[0]
-    fill(ext, low[0], 0, 64, 64)
+def fourth_near(grad, w, first, last, ext):
+    depth, height = grad.shape[:2]
     for d in range(depth):
-        fill(ext, grad[d], d + 1, 64, 64)
-    fill(ext, high[0], depth + 1, 64, 64)
+        fill(ext, grad[d], d, 64, 64)
+    step = height // 2
+
+    @pl.loop(0, 2)
+    def _(block):
+        h0 = block * step
+        for d, dz, side in ((0, 2, first), (depth - 1, 0, last)):
+            left = window(ext, d - dz, h0, step, [dz])
+            value = nt(left, w[:, of_steps([dz], ext.shape[3])])
+            side[0, pl.ds(h0, step)] = value.astype(BF16).reshape(step, -1, LANES)
 
 
 def fourth_part(w, out, ext, block):
@@ -280,7 +289,9 @@
     step = height // 2
     h0 = block * step
     for d in range(depth):
-        value = nt(window(ext, d, h0, step), w[...])
+        own, _ = split_steps(d, depth)
+        left = window(ext, d - 1, h0, step, own)
+        value = nt(left, w[:, of_steps(own, ext.shape[3])])
         out[d, pl.ds(h0, step)] = value.reshape(step, g, LANES)
 
 
@@ -292,63 +303,64 @@
 
     def pair(self):
         n = self.net
-        self.copies = [n.move(self.buf.at[1 - n.core], self.got_a, n.other)]
-
-    def end(self):
-        for copy in self.copies:
-            copy.wait()
+        self.copy = n.move(self.buf.at[1 - n.core], self.got_a, n.other)
 
     def samples(self):
         n = self.net
-        self.end()
+        self.copy.wait()
         self.acc[...] = (self.buf[n.core].astype(F32) + self.got_a[...].astype(F32)).astype(BF16)
-        self.copies = [
-            n.move(self.acc.at[to[0]], self.got_b.at[j], to) for j, to in enumerate(n.peers)
-        ]
+        self.sem = n.ticket()
+        for j, to in enumerate(n.peers):
+            n.move(self.acc.at[to[0]], self.got_b.at[j], to, self.sem)
 
     def chips(self):
         n = self.net
+        n.settle(self.got_b, self.sem)
         total = self.acc[n.s].astype(F32)
-        for j, copy in enumerate(self.copies):
-            copy.wait()
+        for j in range(len(n.peers)):
             total = total + self.got_b[j].astype(F32)
         self.mid[...] = total.astype(BF16)
-        self.copies = [
-            n.move(self.mid.at[chip], self.got_c.at[j], to)
-            for j, (chip, to) in enumerate(n.line)
-        ]
+        self.sem = n.ticket()
+        for j, (chip, to) in enumerate(n.line):
+            n.move(self.mid.at[chip], self.got_c.at[j], to, self.sem)
 
     def back_chips(self):
         n = self.net
+        n.settle(self.got_c, self.sem)
         total = self.mid[n.chip].astype(F32)
-        for j, copy in enumerate(self.copies):
-            copy.wait()
+        for j in range(len(n.line)):
             total = total + self.got_c[j].astype(F32)
         here = self.out.at[n.core, n.s, n.chip]
         here[...] = total.astype(BF16)
-        self.copies = [n.move(here, here, to) for _, to in n.line]
-        self.wide = [[n.move(here, here, to)] for to in n.peers]
+        self.sem = n.ticket()
+        for _, to in n.line:
+            n.move(here, here, to, self.sem)
+        self.wide = [n.ticket() for _ in n.peers]
+        for k, to in enumerate(n.peers):
+            n.move(here, here, to, self.wide[k])
 
     def back_samples(self):
         n = self.net
         chips = len(n.line) + 1
-        for j, copy in enumerate(self.copies):
-            copy.wait()
-            source = lax.rem(n.chip + chips - 1 - j, chips)
-            here = self.out.at[n.core, n.s, source]
+        n.settle(self.got_c, self.sem)
+        for j in range(chips - 1):
+            here = self.out.at[n.core, n.s, lax.rem(n.chip + chips - 1 - j, chips)]
             for k, to in enumerate(n.peers):
-                self.wide[k].append(n.move(here, here, to))
+                n.move(here, here, to, self.wide[k])
 
     def back_pair(self):
         n = self.net
+        samples = len(n.peers) + 1
+        self.sem = n.ticket()
         here = self.out.at[n.core, n.s]
-        self.copies = [n.move(here, here, n.other)]
-        samples = len(n.peers) + 1
-        for k, group in enumerate(self.wide):
-            for copy in group:
-                copy.wait()
+        n.move(here, here, n.other, self.sem)
+        for k, sem in enumerate(self.wide):
             here = self.out.at[n.core, lax.rem(n.s + samples - 1 - k, samples)]
-            self.copies.append(n.move(here, here, n.other))
+            n.settle(here, sem)
+            n.move(here, here, n.other, self.sem)
+
+    def end(self):
+        self.net.settle(self.out.at[1 - self.net.core], self.sem)
 
 
 class Gather:
@@ -358,32 +370,33 @@
 
     def scatter(self):
         n = self.net
-        self.copies = [
-            n.move(self.buf.at[core, s], self.got_a.at[j], to)
-            for j, (core, s, to) in enumerate(n.plane)
-        ]
+        self.sem = n.ticket()
+        for j, (core, s, to) in enumerate(n.plane):
+            n.move(self.buf.at[core, s], self.got_a.at[j], to, self.sem)
 
     def along(self):
         n = self.net
+        n.settle(self.got_a, self.sem)
         total = self.buf[n.core, n.s].astype(F32)
-        for j, copy in enumerate(self.copies):
-            copy.wait()
+        for j in range(len(n.plane)):
             total = total + self.got_a[j].astype(F32)
         here = self.field.at[n.chip]
         here[...] = total.astype(BF16)
-        self.copies = [n.move(here, here, to) for _, to in n.line]
+        self.sem = n.ticket()
+        for _, to in n.line:
+            n.move(here, here, to, self.sem)
 
     def back(self):
         n = self.net
-        for copy in self.copies:
-            copy.wait()
+        n.settle(self.field.at[1:], self.sem)
         here = self.out.at[n.core, n.s]
         here[...] = jnp.sum(self.field[...].astype(F32), axis=0).astype(BF16)
-        self.copies = [n.move(here, here, to) for _, _, to in n.plane]
+        self.sem = n.ticket()
+        for _, _, to in n.plane:
+            n.move(here, here, to, self.sem)
 
     def end(self):
-        for copy in self.copies:
-            copy.wait()
+        self.net.settle(self.got_a, self.sem)
 
 
 class Net:
@@ -429,22 +442,29 @@
         barrier = pltpu.get_barrier_semaphore()
         pl.semaphore_wait(barrier, 2 + len(self.plane) + len(self.line))
 
-    def make(self, src, dst, to):
-        copy = pltpu.make_async_remote_copy(
+    def ticket(self):
+        self.count += 1
+        return self.count - 1
+
+    def make(self, src, dst, to, sem=None):
+        sem = self.ticket() if sem is None else sem
+        return pltpu.make_async_remote_copy(
             src_ref=src,
             dst_ref=dst,
-            send_sem=self.send.at[self.count],
-            recv_sem=self.recv.at[self.count],
+            send_sem=self.send.at[sem],
+            recv_sem=self.recv.at[sem],
             device_id=to,
             device_id_type=MESH,
         )
-        self.count += 1
-        return copy
-
-    def move(self, src, dst, to):
-        copy = self.make(src, dst, to)
+
+    def move(self, src, dst, to, sem=None):
+        copy = self.make(src, dst, to, sem)
         copy.start()
         return copy
+
+    def settle(self, ref, sem):
+        for of in (self.send, self.recv):
+            pltpu.make_async_copy(ref, ref, of.at[sem]).wait()
 
     def halo(self, first, last, low, high):
         up = self.make(last, low, self.above)
@@ -480,30 +500,27 @@
         return finish
 
 
-def copies_of(samples, space):
-    chips = space // 2
-    four = 2 * (1 + (samples - 1) + 2 * (chips - 1) + chips * (samples - 1) + samples)
-    flat, line = 2 * samples - 1, chips - 1
-    return 2 * 4 + 1 + four + 2 * flat + line + flat + line
+def copies_of(samples):
+    return 4 * 2 + 1 + 2 * (5 + samples - 1) + 3 + 2
 
 
 def share(net, rows, gots):
     def group(src, got, mine, targets):
-        copies = [net.move(src, got.at[mine], to) for to in targets]
+        sem = net.ticket()
+        for to in targets:
+            net.move(src, got.at[mine], to, sem)
         got[mine] = src[...]
-        return copies
+        return sem
 
     samples = gots[0].shape[0] // 2
     mine = net.core * samples + net.s
-    copies = group(rows.at[0], gots[0], mine, [to for _, _, to in net.plane])
+    sem = group(rows.at[0], gots[0], mine, [to for _, _, to in net.plane])
     yield
-    for copy in copies:
-        copy.wait()
+    net.settle(gots[0].at[1:], sem)
     rows[1] = jnp.sum(gots[0][...], axis=0)
-    copies = group(rows.at[1], gots[1], net.chip, [to for _, to in net.line])
+    sem = group(rows.at[1], gots[1], net.chip, [to for _, to in net.line])
     yield
-    for copy in copies:
-        copy.wait()
+    net.settle(gots[1].at[1:], sem)
     rows[2] = jnp.sum(gots[1][...], axis=0)
     yield
 
@@ -515,12 +532,13 @@
     w3, w4, fwd3, fwd4, back3, back4 = refs[:6]
     pre, pooled, ext3, grad4, ext4, grad3, wide4, wide3 = refs[6:14]
     halos = refs[14:22]
+    near = refs[-4:]
     other_tile, rows = refs[22:24]
     gots = refs[24:26]
     parts4 = refs[26:32], refs[32:38]
     part3 = refs[38:41]
     cells, low_cells, high_cells, plane, bias3, bias4 = refs[41:47]
-    send, recv, vol, tile, b3, b4, part, part_fwd, here = refs[47:]
+    send, recv, vol, tile, b3, b4, part, part_fwd, here = refs[47:-4]
     loads = [
         pltpu.make_async_copy(w3_hbm, w3, here.at[0]),
         pltpu.make_async_copy(vol_hbm, vol, here.at[2]),
@@ -573,17 +591,17 @@
     slopes(pre)
     done()
     second_kernel(halos[2], halos[3], fwd4, part_fwd, plane, grad4, rows.at[0], ext4)
-    done = net.halo(grad4, grad4, halos[4], halos[5])
+    third_near(grad4, back4, near[0], near[1], wide4)
+    done = net.halo(near[0], near[1], halos[4], halos[5])
     for four, taps in zip(fours, HALVES):
         wgrad_four(ext4, grad4, four.buf, taps)
         four.pair()
-    third_own(grad4, back4, part, wide4)
+    part[...] = third_step(back4, 1, wide4)
     fours[0].samples()
     place_back(w3, back3, 64)
     fours[1].samples()
     done()
-    third_kernel(halos[4], halos[5], back4, part, pre, grad3, rows.at[0], wide4)
-    done = net.halo(grad3.at[0], grad3.at[depth - 1], halos[6].at[0], halos[7].at[0])
+    third_kernel(halos[4], halos[5], part, pre, grad3, rows.at[0])
     bias_steps = share(net, rows, gots)
     next(bias_steps)
     wgrad_three(ext3, grad3, three.buf, range(0, 3))
@@ -592,24 +610,27 @@
     fours[1].chips()
     wgrad_three(ext3, grad3, three.buf, range(6, 9))
     three.scatter()
-    done()
+    fourth_near(grad3, back3, near[2], near[3], wide3)
     fours[0].back_chips()
-    fourth_fill(grad3, halos[6], halos[7], wide3)
+    done = net.halo(near[2], near[3], halos[6], halos[7])
+    fourth_part(back3, cells, wide3, 0)
     fours[1].back_chips()
     next(bias_steps)
-    fourth_part(back3, cells, wide3, 0)
+    fourth_part(back3, cells, wide3, 1)
     three.along()
-    next(bias_steps)
-    fourth_part(back3, cells, wide3, 1)
+    done()
+    for d, side in ((0, halos[6]), (depth - 1, halos[7])):
+        cells[d] = cells[d] + side[0].astype(F32)
     for d in range(depth):
         for g in range(cells.shape[2]):
             out[d, :, g * LANES : (g + 1) * LANES] = cells[d, :, g, :].astype(BF16)
+    fours[0].back_samples()
+    fours[1].back_samples()
+    three.back()
+    next(bias_steps)
     bsum[...] = rows[2]
-    for four in fours:
-        four.back_samples()
-    three.back()
-    for four in fours:
-        four.back_pair()
+    fours[0].back_pair()
+    fours[1].back_pair()
     for each in (*fours, three):
         each.end()
 
@@ -671,7 +692,7 @@
     half = height // 2
     shape = jax.ShapeDtypeStruct
     vm = pltpu.VMEM
-    copies = copies_of(samples, space)
+    copies = copies_of(samples)
     vmem = pl.BlockSpec(memory_space=pltpu.VMEM)
     far = pl.BlockSpec(memory_space=pltpu.HBM)
     counts = [3 * len(taps) * mid for taps in HALVES]
@@ -698,12 +719,12 @@
             vm((half, groups, wide), BF16),
             vm((3, half + 2, groups, wide), BF16),
             vm((depth, height, groups, wide), BF16),
-            vm((3, half + 2, groups, 4 * LANES), BF16),
-            vm((depth + 2, height + 2, groups, 3 * LANES), BF16),
+            vm((1, half + 2, groups, 4 * LANES), BF16),
+            vm((depth, height + 2, groups, 3 * LANES), BF16),
             *[vm(volume.shape[2:], BF16)] * 2,
             *[vm((half, groups, LANES), BF16)] * 2,
-            *[vm((half, groups, wide), BF16)] * 2,
-            *[vm((1, height, groups, wide), BF16)] * 2,
+            *[vm((half, groups, LANES), BF16)] * 2,
+            *[vm((1, height, groups, LANES), BF16)] * 2,
             vm(tile.shape, BF16),
             vm((3, 8, LANES), F32),
             vm((2 * samples, 8, LANES), F32),
@@ -725,6 +746,8 @@
             vm((half * groups, LANES), F32),
             vm((half * groups, wide), F32),
             pltpu.SemaphoreType.DMA((6,)),
+            *[vm((half, groups, LANES), BF16)] * 2,
+            *[vm((1, height, groups, LANES), BF16)] * 2,
         ],
         compiler_params=pltpu.CompilerParams(
             collective_id=0, has_side_effects=True, vmem_limit_bytes=36 * 2**20

time: 40.7 us -> 38 us (0.934)
  Pallas kernels: 39.9 us -> 37.2 us
    pallas_call x1, Pallas kernels: 38.8 us -> 36 us  [local(): pl.pallas_call(functools.partial(mono_kernel, samples, space), out_shape=...]
where the time goes in v3:
time: 38 us; the launch traced here: 37.8 us
  Pallas kernels  37.2 us (98%)
  between operations  0.64 us (2%)
    pallas_call x1, Pallas kernels, local(): pl.pallas_call(functools.partial(mono_kernel, samples, space), out_shape=...  36 us
    pallas_call x1, Pallas kernels, local(): pl.pallas_call(finish_kernel, out_shape=[raw, shape((27, cin, mid), F32),...  1.19 us

profile of v3, /device:TPU:0, one launch (start us, length us, event | category | flops | bytes accessed | tf_op | source)
XLA Modules:
  0.0 37.8 jit_solution(6113604767052054688)
XLA Ops:
  0.6 36.0 %shard_map.101 = (bf16[2,16,4096]{2,1,0:T(8,128)(2,1)S(1)}, bf16[2,4,4,32,128]{4,3,2,1,0:T(8,128)(2,1)S(1)}, bf16[2,4,4,32,128]{4,3,2,1,0:T(8,128)(2,1)S(1)}, bf...) custom-call(bf16[2,16,4096]{2,1,0:T(8,128)(2,1)} %bitcast.12, bf16[2,4096]{1,0:T(2,128)(2,1)} %bitcast.14, ...), custom_call_target="tpu_custom_call" | custom-call | tf_op jit(solution)/shard_map/pallas_call | solution.py:704
  36.6 1.2 %shard_map.102 = (bf16[2,16,4096]{2,1,0:T(8,128)(2,1)}, f32[27,32,64]{2,1,0:T(8,128)}, f32[27,64,128]{2,1,0:T(8,128)}, f32[1,64]{1,0:T(1,128)}, f32[1,128]{1,0:T(1,128)}) custom-call(bf16[2,16,4096]{2,1,0:T(8,128)(2,1)S(1)} %get-tuple-element.15.grad, bf16[2,4,4,32,128]{4,3,2,1,0:T(8,128)(2,1)S(1)} %get-tuple-element.16.out4a, ...), custom_call_target="tpu_custom_call" | custom-call | tf_op jit(solution)/shard_map/pallas_call | solution.py:761

commit v4 on v3

--- a/solution.py
+++ b/solution.py
@@ -32,15 +32,18 @@
                 fwd[row : row + cin, c * cout : (c + 1) * cout] = wide[tap * 3 + dx]
 
 
-def place_back(wide, back, low_out):
+def place_back(wide, back, low_out, blocks=(0, 0, 0)):
     cin, cout = wide.shape[1], wide.shape[2]
+    per = 3 if max(blocks) else 9
+    unit = back.shape[1] // per
     back[...] = jnp.zeros(back.shape, back.dtype)
     for tap in range(9):
         for dx in range(3):
             for c in range(LANES // cin):
-                col = tap * (back.shape[1] // 9)
+                row = blocks[tap // 3] * LANES + c * cin
+                col = tap % per * unit
                 col += slot_of(c - dx + 1, LANES // cin, cout, 2 * LANES, low_out)
-                back[c * cin : (c + 1) * cin, col : col + cout] = wide[(8 - tap) * 3 + dx]
+                back[row : row + cin, col : col + cout] = wide[(8 - tap) * 3 + dx]
 
 
 def spread(raw, dst):
@@ -239,12 +242,13 @@
 
 def third_near(grad, w, first, last, ext):
     fill(ext, grad[...], 0, LANES, LANES)
-    for dz, side in ((2, first), (0, last)):
-        side[...] = third_step(w, dz, ext).astype(BF16).reshape(side.shape)
-
-
-def third_step(w, dz, ext):
-    return nt(window(ext, -dz, 0, ext.shape[1] - 2, [dz]), w[:, of_steps([dz], ext.shape[3])])
+    value = nt(third_window(ext), w[: 2 * LANES]).astype(BF16)
+    first[...] = value[:, :LANES].reshape(first.shape)
+    last[...] = value[:, LANES:].reshape(last.shape)
+
+
+def third_window(ext):
+    return window(ext, 0, 0, ext.shape[1] - 2, [0])
 
 
 def third_kernel(low, high, part, pre, out, bsum):
@@ -578,7 +582,7 @@
     loads[4].wait()
     place_forward(w4, fwd4, 64)
     second_own(fwd4, bias4, part_fwd, ext4)
-    place_back(w4, back4, 128)
+    place_back(w4, back4, 128, (1, 2, 0))
     loads[5].wait()
     tile_copy.wait()
     odd = net.core == 1
@@ -596,7 +600,7 @@
     for four, taps in zip(fours, HALVES):
         wgrad_four(ext4, grad4, four.buf, taps)
         four.pair()
-    part[...] = third_step(back4, 1, wide4)
+    part[...] = nt(third_window(wide4), back4[2 * LANES :])
     fours[0].samples()
     place_back(w3, back3, 64)
     fours[1].samples()
@@ -604,21 +608,19 @@
     third_kernel(halos[4], halos[5], part, pre, grad3, rows.at[0])
     bias_steps = share(net, rows, gots)
     next(bias_steps)
-    wgrad_three(ext3, grad3, three.buf, range(0, 3))
+    wgrad_three(ext3, grad3, three.buf, range(9))
+    three.scatter()
     fours[0].chips()
-    wgrad_three(ext3, grad3, three.buf, range(3, 6))
+    fourth_near(grad3, back3, near[2], near[3], wide3)
     fours[1].chips()
-    wgrad_three(ext3, grad3, three.buf, range(6, 9))
-    three.scatter()
-    fourth_near(grad3, back3, near[2], near[3], wide3)
+    done = net.halo(near[2], near[3], halos[6], halos[7])
+    next(bias_steps)
+    fourth_part(back3, cells, wide3, 0)
+    fourth_part(back3, cells, wide3, 1)
     fours[0].back_chips()
-    done = net.halo(near[2], near[3], halos[6], halos[7])
-    fourth_part(back3, cells, wide3, 0)
-    fours[1].back_chips()
-    next(bias_steps)
-    fourth_part(back3, cells, wide3, 1)
     three.along()
     done()
+    fours[1].back_chips()
     for d, side in ((0, halos[6]), (depth - 1, halos[7])):
         cells[d] = cells[d] + side[0].astype(F32)
     for d in range(depth):
@@ -635,20 +637,32 @@
         each.end()
 
 
-def finish_kernel(grad, out4a, out4b, out3, bsum, volume, wsum3, wsum4, bsum3, bsum4):
-    volume[...] = grad[...]
+def finish_kernel(grad, out4a, out4b, out3, bsum, *refs):
+    volume, to3, to4, bsum3, bsum4, wsum3, wsum4, sems = refs
+    copies = []
+
+    def send(src, dst):
+        copies.append(pltpu.make_async_copy(src, dst, sems.at[len(copies)]))
+        copies[-1].start()
+
+    send(grad, volume)
     for out4, taps in zip((out4a, out4b), HALVES):
         for place, tap in enumerate(taps):
             for dx in range(3):
                 for k in range(4):
                     rows = kept(out4, (place * 3 + dx) * 4 + k)
                     wsum4[tap * 3 + dx, k * 16 : k * 16 + 16] = rows.astype(F32)
+        span = pl.ds(taps[0] * 3, len(taps) * 3)
+        send(wsum4.at[span], to4.at[span])
     for t in range(27):
         value = kept(out3, t).astype(F32)
         wsum3[t, :16] = value[:, :64]
         wsum3[t, 16:] = pltpu.roll(value, 64, 1)[:, :64]
+    send(wsum3, to3)
     bsum4[...] = bsum[0:1]
     bsum3[...] = bsum[1:2, : bsum3.shape[1]]
+    for copy in copies:
+        copy.wait()
 
 
 def per_of(samples, chips, rows):
@@ -712,7 +726,7 @@
             vm((9 * wide, wide), BF16),
             vm((9 * wide, wide), BF16),
             vm((LANES, 9 * 3 * LANES), BF16),
-            vm((LANES, 9 * 4 * LANES), BF16),
+            vm((3 * LANES, 3 * 4 * LANES), BF16),
             vm((depth, height, groups, wide), F32),
             vm((half, groups, LANES), BF16),
             vm((depth + 2, height + 2, groups, wide), BF16),
@@ -768,7 +782,12 @@
             shape((1, cout), F32),
         ],
         in_specs=[vmem] * 5,
-        out_specs=[vmem] * 5,
+        out_specs=[far] * 3 + [vmem] * 2,
+        scratch_shapes=[
+            vm((27, cin, mid), F32),
+            vm((27, mid, cout), F32),
+            pltpu.SemaphoreType.DMA((4,)),
+        ],
         compiler_params=pltpu.CompilerParams(vmem_limit_bytes=16 * 2**20),
     )(*results)
     return (

time: 38 us -> 37.4 us (0.984)
  Pallas kernels: 37.2 us -> 36.6 us
    pallas_call x1, Pallas kernels: 36 us -> 34.9 us  [local(): pl.pallas_call(functools.partial(mono_kernel, samples, space), out_shape=...]
    pallas_call x1, Pallas kernels: 1.19 us -> 1.7 us  [local(): pl.pallas_call(finish_kernel, out_shape=[raw, shape((27, cin, mid), F32),...]
where the time goes in v4:
time: 37.4 us; the launch traced here: 37.3 us
  Pallas kernels  36.6 us (98%)
  between operations  0.64 us (2%)
    pallas_call x1, Pallas kernels, local(): pl.pallas_call(functools.partial(mono_kernel, samples, space), out_shape=...  34.9 us
    pallas_call x1, Pallas kernels, local(): pl.pallas_call(finish_kernel, out_shape=[raw, shape((27, cin, mid), F32),...  1.7 us

profile of v4, /device:TPU:0, one launch (start us, length us, event | category | flops | bytes accessed | tf_op | source)
XLA Modules:
  0.0 37.3 jit_solution(6037406799743043322)
XLA Ops:
  0.6 34.9 %shard_map.101 = (bf16[2,16,4096]{2,1,0:T(8,128)(2,1)S(1)}, bf16[2,4,4,32,128]{4,3,2,1,0:T(8,128)(2,1)S(1)}, bf16[2,4,4,32,128]{4,3,2,1,0:T(8,128)(2,1)S(1)}, bf...) custom-call(bf16[2,16,4096]{2,1,0:T(8,128)(2,1)} %bitcast.12, bf16[2,4096]{1,0:T(2,128)(2,1)} %bitcast.14, ...), custom_call_target="tpu_custom_call" | custom-call | tf_op jit(solution)/shard_map/pallas_call | solution.py:718
  35.6 1.7 %shard_map.102 = (bf16[2,16,4096]{2,1,0:T(8,128)(2,1)}, f32[27,32,64]{2,1,0:T(8,128)}, f32[27,64,128]{2,1,0:T(8,128)}, f32[1,64]{1,0:T(1,128)}, f32[1,128]{1,0:T(1,128)}) custom-call(bf16[2,16,4096]{2,1,0:T(8,128)(2,1)S(1)} %get-tuple-element.15.grad, bf16[2,4,4,32,128]{4,3,2,1,0:T(8,128)(2,1)S(1)} %get-tuple-element.16.out4a, ...), custom_call_target="tpu_custom_call" | custom-call | tf_op jit(solution)/shard_map/pallas_call | solution.py:775

commit v5 on v4

--- a/solution.py
+++ b/solution.py
@@ -608,61 +608,54 @@
     third_kernel(halos[4], halos[5], part, pre, grad3, rows.at[0])
     bias_steps = share(net, rows, gots)
     next(bias_steps)
-    wgrad_three(ext3, grad3, three.buf, range(9))
+    for dz in range(3):
+
+        @pl.when(net.p >= 0)
+        def _(taps=range(dz * 3, dz * 3 + 3)):
+            wgrad_three(ext3, grad3, three.buf, taps)
+
     three.scatter()
     fours[0].chips()
+    fours[1].chips()
+    next(bias_steps)
     fourth_near(grad3, back3, near[2], near[3], wide3)
-    fours[1].chips()
-    done = net.halo(near[2], near[3], halos[6], halos[7])
-    next(bias_steps)
     fourth_part(back3, cells, wide3, 0)
     fourth_part(back3, cells, wide3, 1)
     fours[0].back_chips()
     three.along()
+    fours[1].back_chips()
+    done = net.halo(near[2], near[3], halos[6], halos[7])
+    fours[0].back_samples()
+    fours[1].back_samples()
+    three.back()
+    next(bias_steps)
+    bsum[...] = rows[2]
     done()
-    fours[1].back_chips()
     for d, side in ((0, halos[6]), (depth - 1, halos[7])):
         cells[d] = cells[d] + side[0].astype(F32)
     for d in range(depth):
         for g in range(cells.shape[2]):
             out[d, :, g * LANES : (g + 1) * LANES] = cells[d, :, g, :].astype(BF16)
-    fours[0].back_samples()
-    fours[1].back_samples()
-    three.back()
-    next(bias_steps)
-    bsum[...] = rows[2]
     fours[0].back_pair()
     fours[1].back_pair()
     for each in (*fours, three):
         each.end()
 
 
-def finish_kernel(grad, out4a, out4b, out3, bsum, *refs):
-    volume, to3, to4, bsum3, bsum4, wsum3, wsum4, sems = refs
-    copies = []
-
-    def send(src, dst):
-        copies.append(pltpu.make_async_copy(src, dst, sems.at[len(copies)]))
-        copies[-1].start()
-
-    send(grad, volume)
+def finish_kernel(grad, out4a, out4b, out3, bsum, volume, wsum3, wsum4, bsum3, bsum4):
+    volume[...] = grad[...]
     for out4, taps in zip((out4a, out4b), HALVES):
         for place, tap in enumerate(taps):
             for dx in range(3):
                 for k in range(4):
                     rows = kept(out4, (place * 3 + dx) * 4 + k)
                     wsum4[tap * 3 + dx, k * 16 : k * 16 + 16] = rows.astype(F32)
-        span = pl.ds(taps[0] * 3, len(taps) * 3)
-        send(wsum4.at[span], to4.at[span])
     for t in range(27):
         value = kept(out3, t).astype(F32)
         wsum3[t, :16] = value[:, :64]
         wsum3[t, 16:] = pltpu.roll(value, 64, 1)[:, :64]
-    send(wsum3, to3)
     bsum4[...] = bsum[0:1]
     bsum3[...] = bsum[1:2, : bsum3.shape[1]]
-    for copy in copies:
-        copy.wait()
 
 
 def per_of(samples, chips, rows):
@@ -782,12 +775,7 @@
             shape((1, cout), F32),
         ],
         in_specs=[vmem] * 5,
-        out_specs=[far] * 3 + [vmem] * 2,
-        scratch_shapes=[
-            vm((27, cin, mid), F32),
-            vm((27, mid, cout), F32),
-            pltpu.SemaphoreType.DMA((4,)),
-        ],
+        out_specs=[vmem] * 5,
         compiler_params=pltpu.CompilerParams(vmem_limit_bytes=16 * 2**20),
     )(*results)
     return (

time: 37.4 us -> 36.7 us (0.981)
  Pallas kernels: 36.6 us -> 35.9 us
    pallas_call x1, Pallas kernels: 1.7 us -> 1.19 us  [local(): pl.pallas_call(finish_kernel, out_shape=[raw, shape((27, cin, mid), F32),...]
where the time goes in v5:
time: 36.7 us; the launch traced here: 36.5 us
  Pallas kernels  35.9 us (98%)
  between operations  0.64 us (2%)
    pallas_call x1, Pallas kernels, local(): pl.pallas_call(functools.partial(mono_kernel, samples, space), out_shape=...  34.7 us
    pallas_call x1, Pallas kernels, local(): pl.pallas_call(finish_kernel, out_shape=[raw, shape((27, cin, mid), F32),...  1.19 us

profile of v5, /device:TPU:0, one launch (start us, length us, event | category | flops | bytes accessed | tf_op | source)
XLA Modules:
  0.0 36.5 jit_solution(1237811833660244580)
XLA Ops:
  0.6 34.7 %shard_map.101 = (bf16[2,16,4096]{2,1,0:T(8,128)(2,1)S(1)}, bf16[2,4,4,32,128]{4,3,2,1,0:T(8,128)(2,1)S(1)}, bf16[2,4,4,32,128]{4,3,2,1,0:T(8,128)(2,1)S(1)}, bf...) custom-call(bf16[2,16,4096]{2,1,0:T(8,128)(2,1)} %bitcast.12, bf16[2,4096]{1,0:T(2,128)(2,1)} %bitcast.14, ...), custom_call_target="tpu_custom_call" | custom-call | tf_op jit(solution)/shard_map/pallas_call | solution.py:711
  35.3 1.2 %shard_map.102 = (bf16[2,16,4096]{2,1,0:T(8,128)(2,1)}, f32[27,32,64]{2,1,0:T(8,128)}, f32[27,64,128]{2,1,0:T(8,128)}, f32[1,64]{1,0:T(1,128)}, f32[1,128]{1,0:T(1,128)}) custom-call(bf16[2,16,4096]{2,1,0:T(8,128)(2,1)S(1)} %get-tuple-element.15.grad, bf16[2,4,4,32,128]{4,3,2,1,0:T(8,128)(2,1)S(1)} %get-tuple-element.16.out4a, ...), custom_call_target="tpu_custom_call" | custom-call | tf_op jit(solution)/shard_map/pallas_call | solution.py:768

commit v6 on v5

--- a/solution.py
+++ b/solution.py
@@ -602,23 +602,19 @@
         four.pair()
     part[...] = nt(third_window(wide4), back4[2 * LANES :])
     fours[0].samples()
+    fours[1].samples()
     place_back(w3, back3, 64)
-    fours[1].samples()
     done()
     third_kernel(halos[4], halos[5], part, pre, grad3, rows.at[0])
     bias_steps = share(net, rows, gots)
     next(bias_steps)
-    for dz in range(3):
-
-        @pl.when(net.p >= 0)
-        def _(taps=range(dz * 3, dz * 3 + 3)):
-            wgrad_three(ext3, grad3, three.buf, taps)
-
+    wgrad_three(ext3, grad3, three.buf, range(0, 7))
+    fours[0].chips()
+    wgrad_three(ext3, grad3, three.buf, range(7, 9))
     three.scatter()
-    fours[0].chips()
     fours[1].chips()
+    fourth_near(grad3, back3, near[2], near[3], wide3)
     next(bias_steps)
-    fourth_near(grad3, back3, near[2], near[3], wide3)
     fourth_part(back3, cells, wide3, 0)
     fourth_part(back3, cells, wide3, 1)
     fours[0].back_chips()
@@ -630,14 +626,14 @@
     three.back()
     next(bias_steps)
     bsum[...] = rows[2]
+    fours[0].back_pair()
+    fours[1].back_pair()
     done()
     for d, side in ((0, halos[6]), (depth - 1, halos[7])):
         cells[d] = cells[d] + side[0].astype(F32)
     for d in range(depth):
         for g in range(cells.shape[2]):
             out[d, :, g * LANES : (g + 1) * LANES] = cells[d, :, g, :].astype(BF16)
-    fours[0].back_pair()
-    fours[1].back_pair()
     for each in (*fours, three):
         each.end()
 

time: 36.7 us -> 36.2 us (0.986)
  Pallas kernels: 35.9 us -> 35.4 us
    pallas_call x1, Pallas kernels: 34.7 us -> 34.2 us  [local(): pl.pallas_call(functools.partial(mono_kernel, samples, space), out_shape=...]
where the time goes in v6:
time: 36.2 us; the launch traced here: 36.1 us
  Pallas kernels  35.4 us (98%)
  between operations  0.64 us (2%)
    pallas_call x1, Pallas kernels, local(): pl.pallas_call(functools.partial(mono_kernel, samples, space), out_shape=...  34.2 us
    pallas_call x1, Pallas kernels, local(): pl.pallas_call(finish_kernel, out_shape=[raw, shape((27, cin, mid), F32),...  1.19 us

profile of v6, /device:TPU:0, one launch (start us, length us, event | category | flops | bytes accessed | tf_op | source)
XLA Modules:
  0.0 36.1 jit_solution(12806952599659057795)
XLA Ops:
  0.6 34.2 %shard_map.101 = (bf16[2,16,4096]{2,1,0:T(8,128)(2,1)S(1)}, bf16[2,4,4,32,128]{4,3,2,1,0:T(8,128)(2,1)S(1)}, bf16[2,4,4,32,128]{4,3,2,1,0:T(8,128)(2,1)S(1)}, bf...) custom-call(bf16[2,16,4096]{2,1,0:T(8,128)(2,1)} %bitcast.12, bf16[2,4096]{1,0:T(2,128)(2,1)} %bitcast.14, ...), custom_call_target="tpu_custom_call" | custom-call | tf_op jit(solution)/shard_map/pallas_call | solution.py:707
  34.9 1.2 %shard_map.102 = (bf16[2,16,4096]{2,1,0:T(8,128)(2,1)}, f32[27,32,64]{2,1,0:T(8,128)}, f32[27,64,128]{2,1,0:T(8,128)}, f32[1,64]{1,0:T(1,128)}, f32[1,128]{1,0:T(1,128)}) custom-call(bf16[2,16,4096]{2,1,0:T(8,128)(2,1)S(1)} %get-tuple-element.15.grad, bf16[2,4,4,32,128]{4,3,2,1,0:T(8,128)(2,1)S(1)} %get-tuple-element.16.out4a, ...), custom_call_target="tpu_custom_call" | custom-call | tf_op jit(solution)/shard_map/pallas_call | solution.py:764

commit v7 on v6

--- a/solution.py
+++ b/solution.py
@@ -593,6 +593,7 @@
     for each in (*fours, three):
         each.buf[...] = jnp.zeros(each.buf.shape, BF16)
     slopes(pre)
+    place_back(w3, back3, 64)
     done()
     second_kernel(halos[2], halos[3], fwd4, part_fwd, plane, grad4, rows.at[0], ext4)
     third_near(grad4, back4, near[0], near[1], wide4)
@@ -600,10 +601,9 @@
     for four, taps in zip(fours, HALVES):
         wgrad_four(ext4, grad4, four.buf, taps)
         four.pair()
-    part[...] = nt(third_window(wide4), back4[2 * LANES :])
     fours[0].samples()
     fours[1].samples()
-    place_back(w3, back3, 64)
+    part[...] = nt(third_window(wide4), back4[2 * LANES :])
     done()
     third_kernel(halos[4], halos[5], part, pre, grad3, rows.at[0])
     bias_steps = share(net, rows, gots)

time: 36.2 us -> 36.2 us (level)
  no operation moved by 1% of the time
where the time goes in v7:
time: 36.2 us; the launch traced here: 36.1 us
  Pallas kernels  35.4 us (98%)
  between operations  0.64 us (2%)
    pallas_call x1, Pallas kernels, local(): pl.pallas_call(functools.partial(mono_kernel, samples, space), out_shape=...  34.2 us
    pallas_call x1, Pallas kernels, local(): pl.pallas_call(finish_kernel, out_shape=[raw, shape((27, cin, mid), F32),...  1.19 us

profile of v7, /device:TPU:0, one launch (start us, length us, event | category | flops | bytes accessed | tf_op | source)
XLA Modules:
  0.0 36.1 jit_solution(10421237603010937170)
XLA Ops:
  0.6 34.2 %shard_map.101 = (bf16[2,16,4096]{2,1,0:T(8,128)(2,1)S(1)}, bf16[2,4,4,32,128]{4,3,2,1,0:T(8,128)(2,1)S(1)}, bf16[2,4,4,32,128]{4,3,2,1,0:T(8,128)(2,1)S(1)}, bf...) custom-call(bf16[2,16,4096]{2,1,0:T(8,128)(2,1)} %bitcast.12, bf16[2,4096]{1,0:T(2,128)(2,1)} %bitcast.14, ...), custom_call_target="tpu_custom_call" | custom-call | tf_op jit(solution)/shard_map/pallas_call | solution.py:707
  34.9 1.2 %shard_map.102 = (bf16[2,16,4096]{2,1,0:T(8,128)(2,1)}, f32[27,32,64]{2,1,0:T(8,128)}, f32[27,64,128]{2,1,0:T(8,128)}, f32[1,64]{1,0:T(1,128)}, f32[1,128]{1,0:T(1,128)}) custom-call(bf16[2,16,4096]{2,1,0:T(8,128)(2,1)S(1)} %get-tuple-element.15.grad, bf16[2,4,4,32,128]{4,3,2,1,0:T(8,128)(2,1)S(1)} %get-tuple-element.16.out4a, ...), custom_call_target="tpu_custom_call" | custom-call | tf_op jit(solution)/shard_map/pallas_call | solution.py:764
